TPU v7x, 32 devices: a whole 2x2x4 slice. The times are simulated.
32 devices in a mesh: row: 4 (over y, x), col: 8 (over z, core).
Axes of the slice: x: 2, y: 2, z: 4, core: 2. Of those that a mesh axis runs over, the one named last changes fastest.
Arguments:
- noise: float32 [2048, 3072], P('row', 'col'), may hold values from -30 to 30
- images: float32 [6144, 3072], P('col', 'row'), may hold values from -6 to 6
- time_index: int32 [2048], P('row'), may hold values from 0 to 999
- w_in: float32 [3072, 3072], P(None, 'col'), may hold values from -0.109375 to 0.109375
- time_gain: float32 [3072], P('col'), may hold values from -5 to 5
- w_out: float32 [3072, 3072], P('col'), may hold values from -0.109375 to 0.109375
Outputs:
- targets: float32 [2048, 3072], P('row', 'col')
- row_pot: float32 [2048], P('row')
- col_pot: float32 [6144], P('col')
- grad_in: float32 [3072, 3072], P('row', 'col')
- grad_time: float32 [3072], P('col')
- grad_out: float32 [3072, 3072], P('col', 'row')
- mse: float32 [], replicated
All inputs are finite; a program needn't handle non-finite values.
Results may differ from a plain program's by a relative error of at most 0.0003.
Values sent between devices are 32-bit elements; how exact they have to be, the bound alone decides.
A program may use at most 128 MiB of HBM per device.

v0:
```python
import jax
import jax.numpy as jnp
from jax import lax
from jax.sharding import PartitionSpec as P

ITERS = 2
TIMES = 1000
EPSILON = 0.01


def merged(array, axis, combine):
    everything = jax.tree.map(lambda part: lax.all_gather(part, axis), array)
    first = jax.tree.map(lambda part: part[0], everything)

    def hop(k, so_far):
        return combine(so_far, jax.tree.map(lambda part: part[k], everything))

    return lax.fori_loop(1, lax.axis_size(axis), hop, first)


def joined(left_pair, right_pair):
    peak = jnp.maximum(left_pair[0], right_pair[0])
    total = left_pair[1] * jnp.exp(left_pair[0] - peak) + right_pair[1] * jnp.exp(
        right_pair[0] - peak
    )
    return (peak, total)


def over_images(logits):
    local_peak = jnp.max(logits, axis=1)
    local_total = jnp.sum(jnp.exp(logits - local_peak[:, None]), axis=1)
    peak, total = merged((local_peak, local_total), "col", joined)
    return (peak, total)


def over_noise(logits):
    local_peak = jnp.max(logits, axis=0)
    local_total = jnp.sum(jnp.exp(logits - local_peak[None, :]), axis=0)
    peak, total = merged((local_peak, local_total), "row", joined)
    return (peak, total)


def body(noise, images, time_index, w_in, time_gain, w_out):
    highest = lax.Precision.HIGHEST
    full_noise = lax.all_gather(noise, "col", axis=1, tiled=True)
    full_images = lax.all_gather(images, "row", axis=1, tiled=True)
    width = full_noise.shape[1]
    noise_count = full_noise.shape[0] * lax.axis_size("row")
    image_count = full_images.shape[0] * lax.axis_size("col")
    noise_norms = jnp.sum(full_noise * full_noise, axis=1)
    image_norms = jnp.sum(full_images * full_images, axis=1)
    cross = lax.dot_general(
        full_noise,
        full_images,
        (((1,), (1,)), ((), ())),
        precision=highest,
        preferred_element_type=jnp.float32,
    )
    scaled = (noise_norms[:, None] + image_norms[None, :] - 2.0 * cross) / (width * EPSILON)
    col_pot = jnp.zeros((full_images.shape[0],), jnp.float32)
    row_pot = jnp.zeros((full_noise.shape[0],), jnp.float32)
    for iteration in range(ITERS):
        peak, total = over_images(col_pot[None, :] - scaled)
        row_pot = jnp.log(jnp.float32(image_count)) - (jnp.log(total) + peak)
        peak, total = over_noise(row_pot[:, None] - scaled)
        col_pot = jnp.log(jnp.float32(noise_count)) - (jnp.log(total) + peak)
    logits = col_pot[None, :] - scaled
    peak, total = over_images(logits)
    weights = jnp.exp(logits - (jnp.log(total) + peak)[:, None])
    partial_value = jnp.dot(
        weights, full_images, precision=highest, preferred_element_type=jnp.float32
    )
    slice_width = noise.shape[1]
    slice_start = lax.axis_index("col") * slice_width
    whole_targets = lax.psum(partial_value, "col")
    targets = lax.dynamic_slice_in_dim(whole_targets, slice_start, slice_width, 1)
    fraction = (time_index.astype(jnp.float32) + 0.5) / TIMES
    mixed = (1.0 - fraction)[:, None] * full_noise + fraction[:, None] * whole_targets
    velocity = whole_targets - full_noise
    pre = (
        jnp.dot(mixed, w_in, precision=highest, preferred_element_type=jnp.float32)
        + fraction[:, None] * time_gain[None, :]
    )
    sigma = jax.nn.sigmoid(pre)
    hidden = pre * sigma
    part_out = jnp.dot(hidden, w_out, precision=highest, preferred_element_type=jnp.float32)
    out = lax.psum(part_out, "col")
    diff = out - velocity
    squared = jnp.sum(diff * diff)
    slope = diff / jnp.sqrt(jnp.float32(noise_count))
    local_out = lax.dot_general(
        hidden,
        slope,
        (((0,), (0,)), ((), ())),
        precision=highest,
        preferred_element_type=jnp.float32,
    )
    back = lax.dot_general(
        slope,
        w_out,
        (((1,), (1,)), ((), ())),
        precision=highest,
        preferred_element_type=jnp.float32,
    )
    dpre = back * sigma * (1.0 + pre * (1.0 - sigma))
    local_in = lax.dot_general(
        mixed, dpre, (((0,), (0,)), ((), ())), precision=highest, preferred_element_type=jnp.float32
    )
    local_time = jnp.sum(fraction[:, None] * dpre, axis=0)
    grad_in, grad_out = (
        lax.psum_scatter(local_in, "row", scatter_dimension=0, tiled=True),
        lax.psum_scatter(local_out, "row", scatter_dimension=1, tiled=True),
    )
    grad_time, squared_all = lax.psum((local_time, squared), "row")
    mse = squared_all / (noise_count * width)
    return (targets, row_pot, col_pot, grad_in, grad_time, grad_out, mse)


def solution(mesh):
    placed = (P("row", "col"), P("col", "row"), P("row"), P(None, "col"), P("col"), P("col", None))
    return jax.shard_map(
        body,
        mesh=mesh,
        in_specs=placed,
        out_specs=(
            P("row", "col"),
            P("row"),
            P("col"),
            P("row", "col"),
            P("col"),
            P("col", "row"),
            P(),
        ),
        check_vma=False,
    )
```

profile of v0, /device:TPU:0, one launch (start us, length us, event | category | flops | bytes accessed | tf_op | source)
XLA Modules:
  0.0 786.1 jit_solution(18099109052659360453)
XLA Ops:
  8.7 68.3 %all-gather.23.cloned.1.call-done = f32[512,3072]{1,0:T(8,128)} async-done(((f32[512,384]{1,0:T(8,128)}), f32[512,3072]{1,0:T(8,128)}) %all-gather.23.cloned.1.call-update) | async-done | bytes 6291472 | tf_op jit(solution)/shard_map/all_gather | solution.py:45
  80.3 93.5 %all-gather.25.cloned.1.call-done = f32[768,3072]{1,0:T(8,128)} async-done(((f32[768,768]{1,0:T(8,128)}), f32[768,3072]{1,0:T(8,128)}) %all-gather.25.cloned.1.call-update) | async-done | bytes 9437200 | tf_op jit(solution)/shard_map/all_gather | solution.py:46
  179.2 18.3 %subtract_reduce_fusion.3 = (f32[512]{0:T(512)S(1)}, f32[512,768]{1,0:T(8,128)S(1)}) fusion(f32[512,3072]{1,0:T(8,128)S(1)} %copy-done, f32[768,3072]{1,0:T(8,128)} %all-gather.25.cloned.1.call-done, f32[768]{0:T(1024)S(1)} %multiply_reduce_fusion, f32[512]{0:T(512)S(1)} %multiply_reduce_fusion.2), kind=kOutput, calls=%fused_computation.38 | convolution fusion | flops 14497873920 | bytes 17308672 | tf_op jit(solution)/shard_map/dot_general | solution.py:52
  197.9 12.8 %all-gather.11 = f32[8,1,512]{2,1,0:T(1,128)S(1)} all-gather(f32[1,1,512]{2,1,0:T(1,128)S(1)} %bitcast.95), channel_id=3, replica_groups=mesh['row'=4,'col'=8] {'col'}, dimensions={0}, use_global_device_ids=true | all-gather | bytes 18432 | tf_op jit(solution)/shard_map/all_gather | solution.py:12
  210.8 12.8 %all-gather.10 = f32[8,1,512]{2,1,0:T(1,128)S(1)} all-gather(f32[1,1,512]{2,1,0:T(1,128)S(1)} %bitcast.93), channel_id=2, replica_groups=mesh['row'=4,'col'=8] {'col'}, dimensions={0}, use_global_device_ids=true | all-gather | bytes 18432 | tf_op jit(solution)/shard_map/all_gather | solution.py:12
  224.5 8.1 %all-gather.13 = f32[4,1,768]{2,1,0:T(1,128)S(1)} all-gather(f32[1,1,768]{2,1,0:T(1,128)S(1)} %reshape.65), channel_id=5, replica_groups=mesh['row'=4,'col'=8] {'row'}, dimensions={0}, use_global_device_ids=true | all-gather | bytes 15360 | tf_op jit(solution)/shard_map/all_gather | solution.py:12
  240.7 12.8 %all-gather.15 = f32[8,1,512]{2,1,0:T(1,128)S(1)} all-gather(f32[1,1,512]{2,1,0:T(1,128)S(1)} %bitcast.94), channel_id=7, replica_groups=mesh['row'=4,'col'=8] {'col'}, dimensions={0}, use_global_device_ids=true | all-gather | bytes 18432 | tf_op jit(solution)/shard_map/all_gather | solution.py:12
  253.5 12.8 %all-gather.14 = f32[8,1,512]{2,1,0:T(1,128)S(1)} all-gather(f32[1,1,512]{2,1,0:T(1,128)S(1)} %bitcast.91), channel_id=6, replica_groups=mesh['row'=4,'col'=8] {'col'}, dimensions={0}, use_global_device_ids=true | all-gather | bytes 18432 | tf_op jit(solution)/shard_map/all_gather | solution.py:12
  267.2 8.1 %all-gather.17 = f32[4,1,768]{2,1,0:T(1,128)S(1)} all-gather(f32[1,1,768]{2,1,0:T(1,128)S(1)} %reshape.73), channel_id=9, replica_groups=mesh['row'=4,'col'=8] {'row'}, dimensions={0}, use_global_device_ids=true | all-gather | bytes 15360 | tf_op jit(solution)/shard_map/all_gather | solution.py:12
  275.4 18.3 %all-gather.16 = f32[4,1,768]{2,1,0:T(1,128)S(1)} all-gather(f32[1,1,768]{2,1,0:T(1,128)S(1)} %reshape.71), channel_id=8, replica_groups=mesh['row'=4,'col'=8] {'row'}, dimensions={0}, use_global_device_ids=true | all-gather | bytes 15360 | tf_op jit(solution)/shard_map/all_gather | solution.py:12
  294.6 12.8 %all-gather.19 = f32[8,1,512]{2,1,0:T(1,128)S(1)} all-gather(f32[1,1,512]{2,1,0:T(1,128)S(1)} %bitcast.96), channel_id=11, replica_groups=mesh['row'=4,'col'=8] {'col'}, dimensions={0}, use_global_device_ids=true | all-gather | bytes 18432 | tf_op jit(solution)/shard_map/all_gather | solution.py:12
  307.3 12.8 %all-gather.18 = f32[8,1,512]{2,1,0:T(1,128)S(1)} all-gather(f32[1,1,512]{2,1,0:T(1,128)S(1)} %bitcast.92), channel_id=10, replica_groups=mesh['row'=4,'col'=8] {'col'}, dimensions={0}, use_global_device_ids=true | all-gather | bytes 18432 | tf_op jit(solution)/shard_map/all_gather | solution.py:12
  320.5 19.3 %fusion.6 = f32[512,3072]{1,0:T(8,128)} fusion(f32[768,3072]{1,0:T(8,128)} %all-gather.25.cloned.1.call-done, f32[512,768]{1,0:T(8,128)S(1)} %get-tuple-element.759, f32[512]{0:T(512)S(1)} %log_add_fusion, f32[768]{0:T(1024)S(1)} %add_subtract_fusion), kind=kOutput, calls=%fused_computation.26 | convolution fusion | flops 14496301056 | bytes 17306624 | tf_op jit(solution)/shard_map/dot_general | solution.py:70
  340.4 133.1 %all-reduce.4.cloned.1.call-done = f32[512,3072]{1,0:T(8,128)} async-done(((f32[512,3072]{1,0:T(8,128)}), f32[512,3072]{1,0:T(8,128)}) %all-reduce.4.cloned.1.call-update) | async-done | bytes 6291472 | tf_op jit(solution)/shard_map/psum | solution.py:75
  473.6 14.6 %convolution_add_fusion = f32[512,384]{1,0:T(8,128)S(1)} fusion(f32[3072,384]{1,0:T(8,128)} %param.19, f32[384]{0:T(512)S(1)} %copy-done.7, f32[512]{0:T(512)S(1)} %get-tuple-element.757, f32[512,3072]{1,0:T(8,128)} %all-reduce.4.cloned.1.call-done, f32[512,3072]{1,0:T(8,128)} %all-gather.23.cloned.1.call-done, f32[512]{0:T(512)S(1)} %get-tuple-element.756), kind=kOutput, calls=%fused_computation.43 | convolution fusion | flops 7252869120 | bytes 18093568 | tf_op jit(solution)/shard_map/dot_general | solution.py:81
  489.1 12.0 %fusion.20 = f32[512,3072]{1,0:T(8,128)} fusion(f32[384,3072]{1,0:T(8,128)S(1)} %bitcast.68, f32[512,384]{1,0:T(8,128)S(1)} %convolution_add_fusion), kind=kOutput, calls=%fused_computation.49 | convolution fusion | flops 7248543744 | bytes 11796480 | tf_op jit(solution)/shard_map/dot_general | solution.py:86
  501.4 136.0 %all-reduce.6.cloned.1.call-done = f32[512,3072]{1,0:T(8,128)} async-done(((f32[512,3072]{1,0:T(8,128)}), f32[512,3072]{1,0:T(8,128)}) %all-reduce.6.cloned.1.call-update) | async-done | bytes 6291472 | tf_op jit(solution)/shard_map/psum | solution.py:87
  637.3 9.5 %multiply_reduce_fusion.1 = (f32[]{:T(128)}, f32[512,3072]{1,0:T(8,128)S(1)}) fusion(f32[512,3072]{1,0:T(8,128)} %all-reduce.6.cloned.1.call-done, f32[512,3072]{1,0:T(8,128)} %all-reduce.4.cloned.1.call-done, f32[512,3072]{1,0:T(8,128)} %all-gather.23.cloned.1.call-done), kind=kLoop, calls=%fused_computation.16 | loop fusion | flops 6291455 | bytes 25165828 | tf_op jit(solution)/shard_map/reduce_sum | solution.py:89
  649.4 10.6 %fusion = f32[384,3072]{1,0:T(8,128)} fusion(f32[512,3072]{1,0:T(8,128)S(1)} %get-tuple-element.745, f32[512,384]{1,0:T(8,128)} %copy-done.2), kind=kOutput, calls=%fused_computation.20 | convolution fusion | flops 7250116608 | bytes 11796480 | tf_op jit(solution)/shard_map/dot_general | solution.py:91
  661.2 14.1 %multiply_reduce_fusion.3 = (f32[384]{0:T(512)S(1)}, f32[512,384]{1,0:T(8,128)S(1)}) fusion(f32[512]{0:T(512)S(1)} %get-tuple-element.757, f32[512,384]{1,0:T(8,128)S(1)} %copy-done.3, f32[384,3072]{1,0:T(8,128)} %param.21, f32[512,3072]{1,0:T(8,128)} %copy-done.1), kind=kOutput, calls=%fused_computation.44 | convolution fusion | flops 7251295744 | bytes 12586496 | tf_op jit(solution)/shard_map/dot_general | solution.py:98
  675.3 15.4 %fusion.26 = f32[3072,384]{1,0:T(8,128)} fusion(f32[512,384]{1,0:T(8,128)S(1)} %get-tuple-element.761, f32[512,3072]{1,0:T(8,128)} %all-reduce.4.cloned.1.call-done, f32[512,3072]{1,0:T(8,128)} %all-gather.23.cloned.1.call-done, f32[512]{0:T(512)S(1)} %get-tuple-element.757, f32[512]{0:T(512)S(1)} %get-tuple-element.756), kind=kOutput, calls=%fused_computation.76 | convolution fusion | flops 7252475904 | bytes 18092032 | tf_op jit(solution)/shard_map/dot_general | solution.py:106
  692.8 10.5 %all-reduce = (f32[384]{0:T(512)}, f32[]{:T(128)}) all-reduce(f32[384]{0:T(512)S(1)} %get-tuple-element.760, f32[]{:T(128)} %get-tuple-element.744), channel_id=1, replica_groups=mesh['row'=4,'col'=8] {'row'}, use_global_device_ids=true, to_apply=%region_26.0 | all-reduce | flops 385 | bytes 3080 | tf_op jit(solution)/shard_map/psum | solution.py:114
  703.9 13.4 %reduce-scatter.5.cloned.1.call-done = f32[384,768]{1,0:T(8,128)} async-done(((f32[384,3072]{1,0:T(8,128)}), f32[384,768]{1,0:T(8,128)}) %reduce-scatter.5.cloned.1.call-update) | async-done | bytes 1179664 | tf_op jit(solution)/shard_map/reduce_scatter | solution.py:112
  717.3 60.4 %reduce-scatter.3.cloned.1.call-done = f32[768,384]{1,0:T(8,128)} async-done(((f32[3072,384]{1,0:T(8,128)}), f32[768,384]{1,0:T(8,128)}) %reduce-scatter.3.cloned.1.call-update) | async-done | bytes 1179664 | tf_op jit(solution)/shard_map/reduce_scatter | solution.py:111
  (135 shorter events, 30.3 us)
Async XLA Ops:
  7.2 69.9 %all-gather.23.cloned.1.call-start = ((), (), s32[]{:S(2)}) async-start(), calls=%async_computation.2 | async-start | bytes 7077888 | tf_op jit(solution)/shard_map/all_gather | solution.py:45
  7.9 165.9 %all-gather.25.cloned.1.call-start = ((), (), s32[]{:S(2)}) async-start(), calls=%async_computation.3 | async-start | bytes 11796480 | tf_op jit(solution)/shard_map/all_gather | solution.py:46
  8.6 464.9 %all-reduce.4.cloned.1.call-start = ((), (), s32[]{:S(2)}) async-start(), calls=%async_computation.4 | async-start | bytes 12582912 | tf_op jit(solution)/shard_map/psum | solution.py:75
  173.8 5.5 copy-start
  266.7 73.1 %copy-start.5 = (f32[512]{0:T(512)}, f32[512]{0:T(512)S(1)}, u32[]{:S(2)}) copy-start(f32[512]{0:T(512)S(1)} %add_subtract_fusion.2) | copy-start | bytes 6148
  293.9 45.8 %copy-start.4 = (f32[768]{0:T(1024)}, f32[768]{0:T(1024)S(1)}, u32[]{:S(2)}) copy-start(f32[768]{0:T(1024)S(1)} %add_subtract_fusion) | copy-start | bytes 9220
  339.8 0.7 copy-start.6
  339.8 133.8 %copy-start.7 = (f32[384]{0:T(512)S(1)}, f32[384]{0:T(512)}, u32[]{:S(2)}) copy-start(f32[384]{0:T(512)} %param.20) | copy-start | bytes 4612
  339.8 149.3 %slice-start = ((s8[4718592]{0:T(1024)(128)(4,1)}), s8[524288]{0:T(1024)(128)(4,1)S(1)}, s32[]{:S(2)}) async-start(s8[4718592]{0:T(1024)(128)(4,1)} %bitcast.67), calls=%async_computation.8 | async-start | bytes 1048576
  339.8 297.5 %all-reduce.6.cloned.1.call-start = ((), (), s32[]{:S(2)}) async-start(), calls=%async_computation.5 | async-start | bytes 12582912 | tf_op jit(solution)/shard_map/psum | solution.py:87
  473.6 15.5 %slice-start.1 = ((s8[4718592]{0:T(1024)(128)(4,1)}), s8[4194304]{0:T(1024)(128)(4,1)S(1)}, s32[]{:S(2)}) async-start(s8[4718592]{0:T(1024)(128)(4,1)} %bitcast.67), calls=%async_computation.9 | async-start | bytes 8388608
  488.2 0.9 copy-start.2
  501.1 216.2 %reduce-scatter.5.cloned.1.call-start = ((), (), s32[]{:S(2)}) async-start(), calls=%async_computation.7 | async-start | bytes 5898240 | tf_op jit(solution)/shard_map/reduce_scatter | solution.py:112
  646.8 2.6 copy-start.1
  660.1 1.1 copy-start.3
  660.1 117.6 %reduce-scatter.3.cloned.1.call-start = ((), (), s32[]{:S(2)}) async-start(), calls=%async_computation.6 | async-start | bytes 5898240 | tf_op jit(solution)/shard_map/reduce_scatter | solution.py:111
Sparse Core Ops, SparseCore 0:
  9.6 67.4 all-gather.22
  78.9 94.8 all-gather.24
  339.9 133.6 all-reduce.3
  501.2 136.0 all-reduce.5
  660.2 57.0 reduce-scatter.4
  720.7 56.9 reduce-scatter.2
where the time goes:
time: 794 us; the launch traced here: 786 us
  waiting for transfers between devices  506 us (64%)
  blocking collectives  129 us (16%)
  matrix products  104 us (13%)
  other arithmetic  20.5 us (3%)
  between operations  16.6 us (2%)
  local copies, waits for them, and re-layouts  8.41 us (1%)
    psum x1, waiting for transfers between devices, body(): out = lax.psum(part_out, 'col')  136 us
    psum x1, waiting for transfers between devices, body(): whole_targets = lax.psum(partial_value, 'col')  133 us
    all_gather x10, blocking collectives, merged(): everything = jax.tree.map(lambda part: lax.all_gather(part, axis), array)  118 us
    all_gather x1, waiting for transfers between devices, body(): full_images = lax.all_gather(images, 'row', axis=1, tiled=True)  93.5 us
    all_gather x1, waiting for transfers between devices, body(): full_noise = lax.all_gather(noise, 'col', axis=1, tiled=True)  68.3 us
    reduce_scatter x1, waiting for transfers between devices, body(): lax.psum_scatter(local_in, 'row', scatter_dimension=0, tiled=True)  60.4 us
    dot_general x1, matrix products, body(): jnp.dot(weights, full_images, precision=highest, preferred_element_type=j...  19.3 us
    dot_general x1, matrix products, body(): lax.dot_general(full_noise, full_images, (((1,), (1,)), ((), ())), precis...  18.3 us
  transfers between devices with their start and end apart: 6, of which 6 were waited for; matrix products, arithmetic and copies ran while one was open for 4% of the time, Pallas kernels for 0%

commit v1 on v0

--- a/solution.py
+++ b/solution.py
@@ -1,3 +1,4 @@
+import functools
 import jax
 import jax.numpy as jnp
 from jax import lax
@@ -6,6 +7,19 @@
 ITERS = 2
 TIMES = 1000
 EPSILON = 0.01
+
+
+def teams_work(u, device_axis):
+    many = lax.psum(1, device_axis)
+    front, kept_arr = (u, 0)
+    while 1 << kept_arr < many:
+        b_now = lax.ppermute(front, device_axis, [(q, q ^ 1 << kept_arr) for q in range(many)])
+        front = front + b_now
+        kept_arr = kept_arr + 1
+    return front
+
+
+measure_array_by_axis = functools.partial(teams_work, device_axis="col")
 
 
 def merged(array, axis, combine):
@@ -72,7 +86,7 @@
     )
     slice_width = noise.shape[1]
     slice_start = lax.axis_index("col") * slice_width
-    whole_targets = lax.psum(partial_value, "col")
+    whole_targets = measure_array_by_axis(partial_value)
     targets = lax.dynamic_slice_in_dim(whole_targets, slice_start, slice_width, 1)
     fraction = (time_index.astype(jnp.float32) + 0.5) / TIMES
     mixed = (1.0 - fraction)[:, None] * full_noise + fraction[:, None] * whole_targets

time: 794 us -> 1080 us (1.36)
  waiting for transfers between devices: 506 us -> 790 us
  blocking collectives: 129 us -> 118 us
    ppermute x0 -> x3, waiting for transfers between devices: none -> 419 us  [teams_work(): lax.ppermute(front, device_axis, [(q, q ^ 1 << kept_arr) for q in range(m...]
    psum x1 -> x0, waiting for transfers between devices: 133 us -> none  [body(): whole_targets = lax.psum(partial_value, 'col')]
    all_gather x10, blocking collectives: 118 us -> 108 us  [merged(): everything = jax.tree.map(lambda part: lax.all_gather(part, axis), array)]
  transfers between devices with their start and end apart: 6 -> 8, of which waited for: 6 -> 8; matrix products, arithmetic and copies ran while one was open for 4% -> 3% of each run, Pallas kernels for 0% -> 0%
where the time goes in v1:
time: 1080 us; the launch traced here: 1070 us
  waiting for transfers between devices  790 us (73%)
  blocking collectives  118 us (11%)
  matrix products  107 us (10%)
  other arithmetic  27.6 us (3%)
  between operations  16.1 us (1%)
    ppermute x3, waiting for transfers between devices, teams_work(): lax.ppermute(front, device_axis, [(q, q ^ 1 << kept_arr) for q in range(m...  419 us
    psum x1, waiting for transfers between devices, body(): out = lax.psum(part_out, 'col')  134 us
    all_gather x10, blocking collectives, merged(): everything = jax.tree.map(lambda part: lax.all_gather(part, axis), array)  108 us
    all_gather x1, waiting for transfers between devices, body(): full_images = lax.all_gather(images, 'row', axis=1, tiled=True)  93.5 us
    all_gather x1, waiting for transfers between devices, body(): full_noise = lax.all_gather(noise, 'col', axis=1, tiled=True)  68.3 us
    reduce_scatter x1, waiting for transfers between devices, body(): lax.psum_scatter(local_in, 'row', scatter_dimension=0, tiled=True)  60.4 us
  transfers between devices with their start and end apart: 8, of which 8 were waited for; matrix products, arithmetic and copies ran while one was open for 3% of the time, Pallas kernels for 0%

profile of v1, /device:TPU:0, one launch (start us, length us, event | category | flops | bytes accessed | tf_op | source)
XLA Modules:
  0.0 1068.6 jit_solution(2976093904443865137)
XLA Ops:
  8.7 68.3 %all-gather.23.cloned.1.call-done = f32[512,3072]{1,0:T(8,128)} async-done(((f32[512,384]{1,0:T(8,128)}), f32[512,3072]{1,0:T(8,128)}) %all-gather.23.cloned.1.call-update) | async-done | bytes 6291472 | tf_op jit(solution)/shard_map/all_gather | solution.py:59
  80.3 93.5 %all-gather.25.cloned.1.call-done = f32[768,3072]{1,0:T(8,128)} async-done(((f32[768,768]{1,0:T(8,128)}), f32[768,3072]{1,0:T(8,128)}) %all-gather.25.cloned.1.call-update) | async-done | bytes 9437200 | tf_op jit(solution)/shard_map/all_gather | solution.py:60
  179.2 18.3 %subtract_reduce_fusion.3 = (f32[512]{0:T(512)S(1)}, f32[512,768]{1,0:T(8,128)S(1)}) fusion(f32[512,3072]{1,0:T(8,128)S(1)} %copy-done.1, f32[768,3072]{1,0:T(8,128)} %all-gather.25.cloned.1.call-done, f32[768]{0:T(1024)S(1)} %multiply_reduce_fusion, f32[512]{0:T(512)S(1)} %multiply_reduce_fusion.2), kind=kOutput, calls=%fused_computation.38 | convolution fusion | flops 14497873920 | bytes 17308672 | tf_op jit(solution)/shard_map/dot_general | solution.py:66
  197.9 12.8 %all-gather.11 = f32[8,1,512]{2,1,0:T(1,128)S(1)} all-gather(f32[1,1,512]{2,1,0:T(1,128)S(1)} %bitcast.95), channel_id=3, replica_groups=mesh['row'=4,'col'=8] {'col'}, dimensions={0}, use_global_device_ids=true | all-gather | bytes 18432 | tf_op jit(solution)/shard_map/all_gather | solution.py:26
  210.8 12.8 %all-gather.10 = f32[8,1,512]{2,1,0:T(1,128)S(1)} all-gather(f32[1,1,512]{2,1,0:T(1,128)S(1)} %bitcast.93), channel_id=2, replica_groups=mesh['row'=4,'col'=8] {'col'}, dimensions={0}, use_global_device_ids=true | all-gather | bytes 18432 | tf_op jit(solution)/shard_map/all_gather | solution.py:26
  224.5 8.1 all-gather.13
  240.7 12.8 %all-gather.15 = f32[8,1,512]{2,1,0:T(1,128)S(1)} all-gather(f32[1,1,512]{2,1,0:T(1,128)S(1)} %bitcast.94), channel_id=7, replica_groups=mesh['row'=4,'col'=8] {'col'}, dimensions={0}, use_global_device_ids=true | all-gather | bytes 18432 | tf_op jit(solution)/shard_map/all_gather | solution.py:26
  253.5 12.8 %all-gather.14 = f32[8,1,512]{2,1,0:T(1,128)S(1)} all-gather(f32[1,1,512]{2,1,0:T(1,128)S(1)} %bitcast.91), channel_id=6, replica_groups=mesh['row'=4,'col'=8] {'col'}, dimensions={0}, use_global_device_ids=true | all-gather | bytes 18432 | tf_op jit(solution)/shard_map/all_gather | solution.py:26
  283.6 12.8 %all-gather.19 = f32[8,1,512]{2,1,0:T(1,128)S(1)} all-gather(f32[1,1,512]{2,1,0:T(1,128)S(1)} %bitcast.96), channel_id=11, replica_groups=mesh['row'=4,'col'=8] {'col'}, dimensions={0}, use_global_device_ids=true | all-gather | bytes 18432 | tf_op jit(solution)/shard_map/all_gather | solution.py:26
  296.4 12.8 %all-gather.18 = f32[8,1,512]{2,1,0:T(1,128)S(1)} all-gather(f32[1,1,512]{2,1,0:T(1,128)S(1)} %bitcast.92), channel_id=10, replica_groups=mesh['row'=4,'col'=8] {'col'}, dimensions={0}, use_global_device_ids=true | all-gather | bytes 18432 | tf_op jit(solution)/shard_map/all_gather | solution.py:26
  309.6 18.5 %fusion.6 = f32[512,3072]{1,0:T(8,128)S(1)} fusion(f32[768,3072]{1,0:T(8,128)} %all-gather.25.cloned.1.call-done, f32[512,768]{1,0:T(8,128)S(1)} %get-tuple-element.759, f32[512]{0:T(512)S(1)} %log_add_fusion, f32[768]{0:T(1024)S(1)} %add_subtract_fusion), kind=kOutput, calls=%fused_computation.26 | convolution fusion | flops 14496301056 | bytes 17306624 | tf_op jit(solution)/shard_map/dot_general | solution.py:84
  328.5 9.8 collective-permute-done
  340.0 137.8 %collective-permute-done.1 = f32[512,3072]{1,0:T(8,128)S(1)} collective-permute-done((f32[512,3072]{1,0:T(8,128)S(1)}, f32[512,3072]{1,0:T(8,128)S(1)}, u32[]{:S(2)}, u32[]{:S(2)}) %collective-permute-start.1) | collective-permute-done | bytes 6291488 | tf_op jit(solution)/shard_map/ppermute | solution.py:16
  480.5 271.8 %collective-permute-done.2 = f32[512,3072]{1,0:T(8,128)} collective-permute-done((f32[512,3072]{1,0:T(8,128)S(1)}, f32[512,3072]{1,0:T(8,128)}, u32[]{:S(2)}, u32[]{:S(2)}) %collective-permute-start.2) | collective-permute-done | bytes 6291488 | tf_op jit(solution)/shard_map/ppermute | solution.py:16
  756.2 15.7 %convolution_add_fusion = f32[512,384]{1,0:T(8,128)S(1)} fusion(f32[3072,384]{1,0:T(8,128)} %param.19, f32[384]{0:T(512)S(1)} %copy-done.8, f32[512]{0:T(512)S(1)} %get-tuple-element.757, f32[512,3072]{1,0:T(8,128)S(1)} %add.298, f32[512,3072]{1,0:T(8,128)S(1)} %bitcast.68, f32[512]{0:T(512)S(1)} %get-tuple-element.756), kind=kOutput, calls=%fused_computation.43 | convolution fusion | flops 7252869120 | bytes 18093568 | tf_op jit(solution)/shard_map/dot_general | solution.py:95
  772.8 13.7 %fusion.20 = f32[512,3072]{1,0:T(8,128)} fusion(f32[384,3072]{1,0:T(8,128)} %param.21, f32[512,384]{1,0:T(8,128)S(1)} %convolution_add_fusion), kind=kOutput, calls=%fused_computation.49 | convolution fusion | flops 7248543744 | bytes 11796480 | tf_op jit(solution)/shard_map/dot_general | solution.py:100
  786.6 133.7 %all-reduce.3.cloned.1.call-done = f32[512,3072]{1,0:T(8,128)} async-done(((f32[512,3072]{1,0:T(8,128)}), f32[512,3072]{1,0:T(8,128)}) %all-reduce.3.cloned.1.call-update) | async-done | bytes 6291472 | tf_op jit(solution)/shard_map/psum | solution.py:101
  920.3 9.5 multiply_reduce_fusion.1
  932.4 10.7 fusion
  944.2 14.2 %multiply_reduce_fusion.3 = (f32[384]{0:T(512)S(1)}, f32[512,384]{1,0:T(8,128)S(1)}) fusion(f32[512]{0:T(512)S(1)} %get-tuple-element.757, f32[512,384]{1,0:T(8,128)S(1)} %copy-done.4, f32[384,3072]{1,0:T(8,128)} %param.21, f32[512,3072]{1,0:T(8,128)} %copy-done.2), kind=kOutput, calls=%fused_computation.44 | convolution fusion | flops 7251295744 | bytes 12586496 | tf_op jit(solution)/shard_map/dot_general | solution.py:112
  958.5 15.4 %fusion.26 = f32[3072,384]{1,0:T(8,128)} fusion(f32[512,384]{1,0:T(8,128)S(1)} %get-tuple-element.761, f32[512,3072]{1,0:T(8,128)} %copy-done, f32[512,3072]{1,0:T(8,128)} %all-gather.23.cloned.1.call-done, f32[512]{0:T(512)S(1)} %get-tuple-element.757, f32[512]{0:T(512)S(1)} %get-tuple-element.756), kind=kOutput, calls=%fused_computation.76 | convolution fusion | flops 7252475904 | bytes 18092032 | tf_op jit(solution)/shard_map/dot_general | solution.py:120
  976.0 10.5 all-reduce
  987.1 13.2 %reduce-scatter.5.cloned.1.call-done = f32[384,768]{1,0:T(8,128)} async-done(((f32[384,3072]{1,0:T(8,128)}), f32[384,768]{1,0:T(8,128)}) %reduce-scatter.5.cloned.1.call-update) | async-done | bytes 1179664 | tf_op jit(solution)/shard_map/reduce_scatter | solution.py:126
  1000.3 60.4 %reduce-scatter.3.cloned.1.call-done = f32[768,384]{1,0:T(8,128)} async-done(((f32[3072,384]{1,0:T(8,128)}), f32[768,384]{1,0:T(8,128)}) %reduce-scatter.3.cloned.1.call-update) | async-done | bytes 1179664 | tf_op jit(solution)/shard_map/reduce_scatter | solution.py:125
  (143 shorter events, 53.6 us)
Async XLA Ops:
  7.2 69.9 %all-gather.23.cloned.1.call-start = ((), (), s32[]{:S(2)}) async-start(), calls=%async_computation.2 | async-start | bytes 7077888 | tf_op jit(solution)/shard_map/all_gather | solution.py:59
  7.9 165.9 %all-gather.25.cloned.1.call-start = ((), (), s32[]{:S(2)}) async-start(), calls=%async_computation.3 | async-start | bytes 11796480 | tf_op jit(solution)/shard_map/all_gather | solution.py:60
  8.6 911.7 %all-reduce.3.cloned.1.call-start = ((), (), s32[]{:S(2)}) async-start(), calls=%async_computation.4 | async-start | bytes 12582912 | tf_op jit(solution)/shard_map/psum | solution.py:101
  173.8 5.5 copy-start.1
  266.7 61.4 %copy-start.6 = (f32[512]{0:T(512)}, f32[512]{0:T(512)S(1)}, u32[]{:S(2)}) copy-start(f32[512]{0:T(512)S(1)} %add_subtract_fusion.2) | copy-start | bytes 6148
  283.0 45.1 %copy-start.5 = (f32[768]{0:T(1024)}, f32[768]{0:T(1024)S(1)}, u32[]{:S(2)}) copy-start(f32[768]{0:T(1024)S(1)} %add_subtract_fusion) | copy-start | bytes 9220
  328.1 10.2 collective-permute-start
  340.0 140.5 %copy-start.7 = (s32[512]{0:T(512)S(1)}, s32[512]{0:T(512)}, u32[]{:S(2)}) copy-start(s32[512]{0:T(512)} %param.18) | copy-start | bytes 6148
  340.0 137.8 %collective-permute-start.1 = (f32[512,3072]{1,0:T(8,128)S(1)}, f32[512,3072]{1,0:T(8,128)S(1)}, u32[]{:S(2)}, u32[]{:S(2)}) collective-permute-start(f32[512,3072]{1,0:T(8,128)S(1)} %add.296), channel_id=1, source_target_pairs={{0,2},{1,3},{2,0},{3,1},{4,6},{5,7},{6,4},{7,5},{8,10},{9,11},{10,... | collective-permute-start | bytes 18874376 | tf_op jit(solution)/shard_map/ppermute | solution.py:16
  479.4 272.8 %collective-permute-start.2 = (f32[512,3072]{1,0:T(8,128)S(1)}, f32[512,3072]{1,0:T(8,128)}, u32[]{:S(2)}, u32[]{:S(2)}) collective-permute-start(f32[512,3072]{1,0:T(8,128)S(1)} %add.297), channel_id=1, source_target_pairs={{0,4},{1,5},{2,6},{3,7},{4,0},{5,1},{6,2},{7,3},{8,12},{9,13},{10,... | collective-permute-start | bytes 18874376 | tf_op jit(solution)/shard_map/ppermute | solution.py:16
  480.4 275.7 %slice-start = ((s8[6291456]{0:T(1024)(128)(4,1)}), s8[4194304]{0:T(1024)(128)(4,1)S(1)}, s32[]{:S(2)}) async-start(s8[6291456]{0:T(1024)(128)(4,1)} %bitcast.67), calls=%async_computation.7 | async-start | bytes 8388608
  480.4 275.7 %slice-start.1 = ((s8[6291456]{0:T(1024)(128)(4,1)}), s8[2097152]{0:T(1024)(128)(4,1)S(1)}, s32[]{:S(2)}) async-start(s8[6291456]{0:T(1024)(128)(4,1)} %bitcast.67), calls=%async_computation.8 | async-start | bytes 4194304
  480.4 275.7 %copy-start.8 = (f32[384]{0:T(512)S(1)}, f32[384]{0:T(512)}, u32[]{:S(2)}) copy-start(f32[384]{0:T(512)} %param.20) | copy-start | bytes 4612
  756.1 15.8 %copy-start = (f32[512,3072]{1,0:T(8,128)}, f32[512,3072]{1,0:T(8,128)S(1)}, u32[]{:S(2)}) copy-start(f32[512,3072]{1,0:T(8,128)S(1)} %add.298) | copy-start | bytes 18874372
  771.9 0.9 copy-start.3
  786.6 213.8 %reduce-scatter.5.cloned.1.call-start = ((), (), s32[]{:S(2)}) async-start(), calls=%async_computation.6 | async-start | bytes 5898240 | tf_op jit(solution)/shard_map/reduce_scatter | solution.py:126
  929.8 2.6 copy-start.2
  943.1 1.1 copy-start.4
  943.1 117.6 %reduce-scatter.3.cloned.1.call-start = ((), (), s32[]{:S(2)}) async-start(), calls=%async_computation.5 | async-start | bytes 5898240 | tf_op jit(solution)/shard_map/reduce_scatter | solution.py:125
Sparse Core Ops, SparseCore 0:
  9.6 67.4 all-gather.22
  78.9 94.8 all-gather.24
  786.7 133.6 all-reduce.2
  943.2 57.0 reduce-scatter.4
  1003.8 56.9 reduce-scatter.2
